TPU v7x, 32 devices: a whole 2x2x4 slice. The times are simulated.
32 devices in a mesh: vocab: 4 (over x, core), fsdp: 8 (over z, y).
Axes of the slice: x: 2, y: 2, z: 4, core: 2. Of those that a mesh axis runs over, the one named last changes fastest.
Arguments:
- hidden: bfloat16 [2, 384, 4096], P(None, 'fsdp'), may hold values from -1000 to 1000
- norm_gain: bfloat16 [4096], replicated, may hold values from 0.5 to 1.5
- labels: int32 [2, 384], P(None, 'fsdp'), may hold values from 0 to 65535
- head_weight: bfloat16 [4096, 65536], P(None, ('vocab', 'fsdp')), may hold values from -1 to 1
- head_ema: float32 [4096, 65536], P(None, ('vocab', 'fsdp')), may hold values from 1e-09 to 0.001
- gain_ema: float32 [4096], replicated, may hold values from 0.0001 to 0.03
Outputs:
- head_ema_new: float32 [4096, 65536], P(None, ('vocab', 'fsdp'))
- gain_ema_new: float32 [4096], replicated
All inputs are finite; a program needn't handle non-finite values.
Results may differ from a plain program's by a relative error of at most 0.00049.
Values may be sent and summed in bfloat16 or wider, within the bound.
A program may use at most 192 MiB of HBM per device.

v0:
```python
import jax
import jax.numpy as jnp
from jax import lax
from jax.sharding import PartitionSpec as P

BETA = 0.99
EPS = 1e-05


def on_device(hidden, norm_gain, labels, head_weight, head_ema, gain_ema):
    batches, own_rows, features = hidden.shape
    columns = head_weight.shape[1]
    column_ids = lax.iota(jnp.int32, columns)[None, :] + lax.axis_index(("vocab", "fsdp")) * columns
    gain_wide = norm_gain.astype(jnp.float32)
    wide = hidden.astype(jnp.float32)
    factor = lax.rsqrt(jnp.mean(wide * wide, axis=-1, keepdims=True) + EPS)
    scaled = (wide * factor * gain_wide).astype(jnp.bfloat16)
    count = batches * own_rows * lax.axis_size("fsdp")
    gradient = jnp.zeros((features, columns), jnp.float32)
    for batch in range(batches):
        batch_rows = scaled[batch]
        batch_labels = labels[batch]
        rows_all, labels_all = (
            lax.all_gather(batch_rows, "fsdp", axis=0, tiled=True),
            lax.all_gather(batch_labels, "fsdp", axis=0, tiled=True),
        )
        logits = jnp.dot(rows_all, head_weight, preferred_element_type=jnp.float32)
        local_top = jnp.max(logits, axis=1)
        row_top = lax.pmax(local_top, ("vocab", "fsdp"))
        local_total = jnp.sum(jnp.exp(logits - row_top[:, None]), axis=1)
        row_total = lax.psum(local_total, ("vocab", "fsdp"))
        chances = jnp.exp(logits - row_top[:, None]) / row_total[:, None]
        hits = (labels_all[:, None] == column_ids).astype(jnp.float32)
        slope = (chances - hits).astype(jnp.bfloat16)
        gradient = gradient + lax.dot_general(
            rows_all, slope, (((0,), (0,)), ((), ())), preferred_element_type=jnp.float32
        )
    head_new = BETA * head_ema + (1.0 - BETA) * gradient * gradient / count
    partial_sum = jnp.sum(head_weight.astype(jnp.float32) * gradient, axis=1)
    gain_grad = lax.psum(partial_sum, ("vocab", "fsdp")) / gain_wide
    gain_new = BETA * gain_ema + (1.0 - BETA) * gain_grad * gain_grad / count
    return (head_new, gain_new)


def solution(mesh):
    return jax.shard_map(
        on_device,
        mesh=mesh,
        in_specs=(
            P(None, "fsdp", None),
            P(),
            P(None, "fsdp"),
            P(None, ("vocab", "fsdp")),
            P(None, ("vocab", "fsdp")),
            P(),
        ),
        out_specs=(P(None, ("vocab", "fsdp")), P()),
        check_vma=False,
    )
```

profile of v0, /device:TPU:0, one launch (start us, length us, event | category | flops | bytes accessed | tf_op | source)
XLA Modules:
  0.0 369.3 jit_solution(13150943076576442699)
XLA Ops:
  7.2 0.0 all-gather.7.cloned.1.call-start
  7.2 1.4 fusion.11
  8.6 0.7 convert_element_type.25
  9.3 1.4 fusion.13
  10.7 0.9 fusion.24
  11.6 0.0 all-gather.7.cloned.1.call-update
  11.7 0.0 all-gather.9.cloned.1.call-start
  11.7 0.7 all-gather.9.cloned.1.call-update
  12.4 21.0 %copy.9 = bf16[4096,2048]{0,1:T(8,128)(2,1)} copy(bf16[4096,2048]{1,0:T(8,128)(2,1)} %param.9) | data formatting | bytes 33554432 | tf_op args[3]
  33.4 0.0 copy-start.3
  33.4 0.0 copy-start.2
  33.4 31.2 %copy.8 = f32[4096,2048]{0,1:T(8,128)} copy(f32[4096,2048]{1,0:T(8,128)} %param.10) | data formatting | bytes 67108864 | tf_op args[4]
  64.6 0.0 copy-done.3
  64.6 0.6 dynamic-slice
  65.8 0.0 copy-done.2
  65.9 0.1 bitcast_dynamic-update-slice_fusion.1
  66.0 0.1 bitcast_dynamic-update-slice_fusion
  66.0 13.1 %all-reduce.2 = (s32[384]{0:T(512)S(1)}, s32[384]{0:T(512)S(1)}) all-reduce(s32[384]{0:T(512)S(1)} %bitcast_dynamic-update-slice_fusion.1, s32[384]{0:T(512)S(1)} %bitcast_dynamic-update-slice_fusion), channel_id=3, replica_groups=mesh['vocab'=4,'fsdp'=8] {'fsdp'}, use_global_device_ids=true, to_apply=%add | all-reduce | flops 768 | bytes 6144
  79.1 0.0 all-gather.7.cloned.1.call-done
  79.1 11.5 %fusion.25 = (f32[384]{0:T(512)S(1)}, f32[384,2048]{1,0:T(8,128)S(1)}) fusion(bf16[4096,2048]{1,0:T(8,128)(2,1)} %param.9, bf16[1,384,4096]{2,1,0:T(8,128)(2,1)} %all-gather.7.cloned.1.call-done), kind=kOutput, calls=%fused_computation.39 | convolution fusion | flops 6443236864 | bytes 23070208 | tf_op jit(solution)/shard_map/dot_general | solution.py:27
  90.6 44.9 %all-gather.9.cloned.1.call-done = bf16[1,384,4096]{2,1,0:T(8,128)(2,1)} async-done(((bf16[1,48,4096]{2,1,0:T(8,128)(2,1)}), bf16[1,384,4096]{2,1,0:T(8,128)(2,1)}) %all-gather.9.cloned.1.call-update) | async-done | bytes 3145744 | tf_op jit(solution)/shard_map/all_gather | solution.py:24
  135.5 12.3 %fusion.26 = (f32[384]{0:T(512)S(1)}, f32[384,2048]{1,0:T(8,128)}) fusion(bf16[4096,2048]{1,0:T(8,128)(2,1)} %param.9, bf16[1,384,4096]{2,1,0:T(8,128)(2,1)} %all-gather.9.cloned.1.call-done), kind=kOutput, calls=%fused_computation.40 | convolution fusion | flops 6443236864 | bytes 23070208 | tf_op jit(solution)/shard_map/dot_general | solution.py:27
  147.8 39.2 %all-reduce.4 = (f32[384]{0:T(512)S(1)}, f32[384]{0:T(512)S(1)}) all-reduce(f32[384]{0:T(512)S(1)} %get-tuple-element.14, f32[384]{0:T(512)S(1)} %get-tuple-element.16), channel_id=1, replica_groups=mesh['vocab'=4,'fsdp'=8] {'vocab','fsdp'}, use_global_device_ids=true, to_apply=%region_2.0 | all-reduce | flops 768 | bytes 6144 | tf_op jit(solution)/shard_map/pmax | solution.py:29
  187.0 2.9 fusion.9
  189.9 40.1 %all-reduce.3 = (f32[384]{0:T(512)S(1)}, f32[384]{0:T(512)S(1)}) all-reduce(f32[384]{0:T(512)S(1)} %get-tuple-element.18, f32[384]{0:T(512)S(1)} %get-tuple-element.19), channel_id=1, replica_groups=mesh['vocab'=4,'fsdp'=8] {'vocab','fsdp'}, use_global_device_ids=true, to_apply=%region_4.0 | all-reduce | flops 768 | bytes 6144 | tf_op jit(solution)/shard_map/psum | solution.py:31
  229.9 17.4 %fusion.5 = f32[4096,2048]{0,1:T(8,128)} fusion(bf16[1,384,4096]{2,1,0:T(8,128)(2,1)} %all-gather.7.cloned.1.call-done, f32[384,2048]{1,0:T(8,128)S(1)} %get-tuple-element.15, s32[2048]{0:T(1024)S(1)} %iota_add_fusion, f32[384]{0:T(512)S(1)} %get-tuple-element.6, f32[384]{0:T(512)S(1)} %get-tuple-element.8, s32[384]{0:T(512)S(1)} %get-tuple-element.4), kind=kOutput, calls=%fused_computation.8 | convolution fusion | flops 6447169536 | bytes 39858688 | tf_op jit(solution)/shard_map/dot_general | solution.py:35
  247.3 41.1 %multiply_reduce_fusion = (f32[4096]{0:T(1024)S(1)}, f32[4096,2048]{0,1:T(8,128)}) fusion(bf16[4096,2048]{0,1:T(8,128)(2,1)} %copy.9, f32[4096,2048]{0,1:T(8,128)} %copy.8, f32[4096,2048]{0,1:T(8,128)} %fusion.5, f32[384,2048]{1,0:T(8,128)} %get-tuple-element.17, f32[384]{0:T(512)S(1)} %get-tuple-element.7, f32[384]{0:T(512)S(1)} %get-tuple-element.9, ...), kind=kOutput, calls=%fused_computation.3 | convolution fusion | flops 6522662912 | bytes 123761152 | tf_op jit(solution)/shard_map/dot_general | solution.py:35
  288.4 40.1 %psum.23 = f32[4096]{0:T(1024)S(1)} all-reduce(f32[4096]{0:T(1024)S(1)} %get-tuple-element.10), channel_id=1, replica_groups=mesh['vocab'=4,'fsdp'=8] {'vocab','fsdp'}, use_global_device_ids=true, to_apply=%region_10.0 | all-reduce | flops 4096 | bytes 32768 | tf_op jit(solution)/shard_map/psum | solution.py:40
  328.5 0.0 copy-start
  328.5 0.0 copy-start.1
  328.5 33.4 %copy.10 = f32[4096,2048]{1,0:T(8,128)} copy(f32[4096,2048]{0,1:T(8,128)} %get-tuple-element.11) | data formatting | bytes 67108864
  361.9 0.0 copy-done
  361.9 0.0 copy-done.1
  361.9 0.6 fusion.23
  (4 shorter events, 0.0 us)
Async XLA Ops:
  7.2 72.0 %all-gather.7.cloned.1.call-start = ((), (), s32[]{:S(2)}) async-start(), calls=%async_computation | async-start | bytes 3538944 | tf_op jit(solution)/shard_map/all_gather | solution.py:24
  11.7 123.8 %all-gather.9.cloned.1.call-start = ((), (), s32[]{:S(2)}) async-start(), calls=%async_computation.1 | async-start | bytes 3538944 | tf_op jit(solution)/shard_map/all_gather | solution.py:24
  33.4 31.2 %copy-start.3 = (u32[32]{0:T(128)S(1)}, u32[32]{0:T(128)}, u32[]{:S(2)}) copy-start(u32[32]{0:T(128)} %constant.34) | copy-start | bytes 388
  33.4 32.4 %copy-start.2 = (s32[2,48]{1,0:T(2,128)S(1)}, s32[2,48]{1,0:T(2,128)}, u32[]{:S(2)}) copy-start(s32[2,48]{1,0:T(2,128)} %param.8) | copy-start | bytes 1156
  328.5 33.4 %copy-start = (bf16[4096]{0:T(1024)(128)(2,1)S(1)}, bf16[4096]{0:T(1024)(128)(2,1)}, u32[]{:S(2)}) copy-start(bf16[4096]{0:T(1024)(128)(2,1)} %param.7) | copy-start | bytes 24580
  328.5 33.4 %copy-start.1 = (f32[4096]{0:T(1024)S(1)}, f32[4096]{0:T(1024)}, u32[]{:S(2)}) copy-start(f32[4096]{0:T(1024)} %param.11) | copy-start | bytes 49156
Sparse Core Ops, SparseCore 0:
  11.8 62.7 all-gather.6
  76.7 58.7 all-gather.8
where the time goes:
time: 371 us; the launch traced here: 369 us
  blocking collectives  132 us (36%)
  local copies, waits for them, and re-layouts  87.3 us (24%)
  matrix products  82.3 us (22%)
  waiting for transfers between devices  45.6 us (12%)
  between operations  14.7 us (4%)
  other arithmetic  6.97 us (2%)
    unnamed x16, local copies, waits for them, and re-layouts  86.3 us
    dot_general x2, matrix products, on_device(): lax.dot_general(rows_all, slope, (((0,), (0,)), ((), ())), preferred_elem...  58.5 us
    all_gather x2, waiting for transfers between devices, on_device(): lax.all_gather(batch_rows, 'fsdp', axis=0, tiled=True)  44.9 us
    psum x1, blocking collectives, on_device(): row_total = lax.psum(local_total, ('vocab', 'fsdp'))  40.1 us
    psum x1, blocking collectives, on_device(): gain_grad = lax.psum(partial_sum, ('vocab', 'fsdp')) / gain_wide  40.1 us
    pmax x1, blocking collectives, on_device(): row_top = lax.pmax(local_top, ('vocab', 'fsdp'))  39.2 us
    dot_general x2, matrix products, on_device(): logits = jnp.dot(rows_all, head_weight, preferred_element_type=jnp.float32)  23.8 us
    unnamed x1, blocking collectives  13.1 us
  transfers between devices with their start and end apart: 2, of which 1 were waited for; matrix products, arithmetic and copies ran while one was open for 17% of the time, Pallas kernels for 0%

commit v1 on v0

--- a/solution.py
+++ b/solution.py
@@ -37,7 +37,7 @@
         )
     head_new = BETA * head_ema + (1.0 - BETA) * gradient * gradient / count
     partial_sum = jnp.sum(head_weight.astype(jnp.float32) * gradient, axis=1)
-    gain_grad = lax.psum(partial_sum, ("vocab", "fsdp")) / gain_wide
+    gain_grad = lax.psum(lax.psum(partial_sum, "fsdp"), "vocab") / gain_wide
     gain_new = BETA * gain_ema + (1.0 - BETA) * gain_grad * gain_grad / count
     return (head_new, gain_new)
 

time: 371 us -> 378 us (1.019)
  blocking collectives: 132 us -> 139 us
    psum x1 -> x2, blocking collectives: 40.1 us -> 46.8 us  [on_device(): gain_grad = lax.psum(lax.psum(partial_sum, 'fsdp'), 'vocab') / gain_wide]
where the time goes in v1:
time: 378 us; the launch traced here: 376 us
  blocking collectives  139 us (37%)
  local copies, waits for them, and re-layouts  87.3 us (23%)
  matrix products  82.3 us (22%)
  waiting for transfers between devices  45.6 us (12%)
  between operations  14.8 us (4%)
  other arithmetic  6.97 us (2%)
    unnamed x16, local copies, waits for them, and re-layouts  86.3 us
    dot_general x2, matrix products, on_device(): lax.dot_general(rows_all, slope, (((0,), (0,)), ((), ())), preferred_elem...  58.5 us
    psum x2, blocking collectives, on_device(): gain_grad = lax.psum(lax.psum(partial_sum, 'fsdp'), 'vocab') / gain_wide  46.8 us
    all_gather x2, waiting for transfers between devices, on_device(): lax.all_gather(batch_rows, 'fsdp', axis=0, tiled=True)  44.9 us
    psum x1, blocking collectives, on_device(): row_total = lax.psum(local_total, ('vocab', 'fsdp'))  40.1 us
    pmax x1, blocking collectives, on_device(): row_top = lax.pmax(local_top, ('vocab', 'fsdp'))  39.2 us
    dot_general x2, matrix products, on_device(): logits = jnp.dot(rows_all, head_weight, preferred_element_type=jnp.float32)  23.8 us
    unnamed x1, blocking collectives  13.1 us
  transfers between devices with their start and end apart: 2, of which 1 were waited for; matrix products, arithmetic and copies ran while one was open for 17% of the time, Pallas kernels for 0%

profile of v1, /device:TPU:0, one launch (start us, length us, event | category | flops | bytes accessed | tf_op | source)
XLA Modules:
  0.0 376.0 jit_solution(9877657261390933105)
XLA Ops:
  7.2 0.0 all-gather.7.cloned.1.call-start
  7.2 1.4 fusion.11
  8.6 0.7 convert_element_type.25
  9.3 1.4 fusion.13
  10.7 0.9 fusion.24
  11.6 0.0 all-gather.7.cloned.1.call-update
  11.7 0.0 all-gather.9.cloned.1.call-start
  11.7 0.7 all-gather.9.cloned.1.call-update
  12.4 21.0 %copy.9 = bf16[4096,2048]{0,1:T(8,128)(2,1)} copy(bf16[4096,2048]{1,0:T(8,128)(2,1)} %param.9) | data formatting | bytes 33554432 | tf_op args[3]
  33.4 0.0 copy-start.3
  33.4 0.0 copy-start.2
  33.4 31.2 %copy.8 = f32[4096,2048]{0,1:T(8,128)} copy(f32[4096,2048]{1,0:T(8,128)} %param.10) | data formatting | bytes 67108864 | tf_op args[4]
  64.6 0.0 copy-done.3
  64.6 0.6 dynamic-slice
  65.8 0.0 copy-done.2
  65.9 0.1 bitcast_dynamic-update-slice_fusion.1
  66.0 0.1 bitcast_dynamic-update-slice_fusion
  66.0 13.1 %all-reduce.2 = (s32[384]{0:T(512)S(1)}, s32[384]{0:T(512)S(1)}) all-reduce(s32[384]{0:T(512)S(1)} %bitcast_dynamic-update-slice_fusion.1, s32[384]{0:T(512)S(1)} %bitcast_dynamic-update-slice_fusion), channel_id=3, replica_groups=mesh['vocab'=4,'fsdp'=8] {'fsdp'}, use_global_device_ids=true, to_apply=%add | all-reduce | flops 768 | bytes 6144
  79.1 0.0 all-gather.7.cloned.1.call-done
  79.1 11.5 %fusion.25 = (f32[384]{0:T(512)S(1)}, f32[384,2048]{1,0:T(8,128)S(1)}) fusion(bf16[4096,2048]{1,0:T(8,128)(2,1)} %param.9, bf16[1,384,4096]{2,1,0:T(8,128)(2,1)} %all-gather.7.cloned.1.call-done), kind=kOutput, calls=%fused_computation.39 | convolution fusion | flops 6443236864 | bytes 23070208 | tf_op jit(solution)/shard_map/dot_general | solution.py:27
  90.6 44.9 %all-gather.9.cloned.1.call-done = bf16[1,384,4096]{2,1,0:T(8,128)(2,1)} async-done(((bf16[1,48,4096]{2,1,0:T(8,128)(2,1)}), bf16[1,384,4096]{2,1,0:T(8,128)(2,1)}) %all-gather.9.cloned.1.call-update) | async-done | bytes 3145744 | tf_op jit(solution)/shard_map/all_gather | solution.py:24
  135.5 12.3 %fusion.26 = (f32[384]{0:T(512)S(1)}, f32[384,2048]{1,0:T(8,128)}) fusion(bf16[4096,2048]{1,0:T(8,128)(2,1)} %param.9, bf16[1,384,4096]{2,1,0:T(8,128)(2,1)} %all-gather.9.cloned.1.call-done), kind=kOutput, calls=%fused_computation.40 | convolution fusion | flops 6443236864 | bytes 23070208 | tf_op jit(solution)/shard_map/dot_general | solution.py:27
  147.8 39.2 %all-reduce.4 = (f32[384]{0:T(512)S(1)}, f32[384]{0:T(512)S(1)}) all-reduce(f32[384]{0:T(512)S(1)} %get-tuple-element.14, f32[384]{0:T(512)S(1)} %get-tuple-element.16), channel_id=1, replica_groups=mesh['vocab'=4,'fsdp'=8] {'vocab','fsdp'}, use_global_device_ids=true, to_apply=%region_2.0 | all-reduce | flops 768 | bytes 6144 | tf_op jit(solution)/shard_map/pmax | solution.py:29
  187.0 2.9 fusion.9
  189.9 40.1 %all-reduce.3 = (f32[384]{0:T(512)S(1)}, f32[384]{0:T(512)S(1)}) all-reduce(f32[384]{0:T(512)S(1)} %get-tuple-element.18, f32[384]{0:T(512)S(1)} %get-tuple-element.19), channel_id=1, replica_groups=mesh['vocab'=4,'fsdp'=8] {'vocab','fsdp'}, use_global_device_ids=true, to_apply=%region_4.0 | all-reduce | flops 768 | bytes 6144 | tf_op jit(solution)/shard_map/psum | solution.py:31
  229.9 17.4 %fusion.5 = f32[4096,2048]{0,1:T(8,128)} fusion(bf16[1,384,4096]{2,1,0:T(8,128)(2,1)} %all-gather.7.cloned.1.call-done, f32[384,2048]{1,0:T(8,128)S(1)} %get-tuple-element.15, s32[2048]{0:T(1024)S(1)} %iota_add_fusion, f32[384]{0:T(512)S(1)} %get-tuple-element.6, f32[384]{0:T(512)S(1)} %get-tuple-element.8, s32[384]{0:T(512)S(1)} %get-tuple-element.4), kind=kOutput, calls=%fused_computation.8 | convolution fusion | flops 6447169536 | bytes 39858688 | tf_op jit(solution)/shard_map/dot_general | solution.py:35
  247.3 41.1 %multiply_reduce_fusion = (f32[4096]{0:T(1024)S(1)}, f32[4096,2048]{0,1:T(8,128)}) fusion(bf16[4096,2048]{0,1:T(8,128)(2,1)} %copy.9, f32[4096,2048]{0,1:T(8,128)} %copy.8, f32[4096,2048]{0,1:T(8,128)} %fusion.5, f32[384,2048]{1,0:T(8,128)} %get-tuple-element.17, f32[384]{0:T(512)S(1)} %get-tuple-element.7, f32[384]{0:T(512)S(1)} %get-tuple-element.9, ...), kind=kOutput, calls=%fused_computation.3 | convolution fusion | flops 6522662912 | bytes 123761152 | tf_op jit(solution)/shard_map/dot_general | solution.py:35
  288.4 36.5 %psum.30 = f32[4096]{0:T(1024)S(1)} all-reduce(f32[4096]{0:T(1024)S(1)} %get-tuple-element.10), channel_id=1, replica_groups=mesh['vocab'=4,'fsdp'=8] {'fsdp'}, use_global_device_ids=true, to_apply=%region_10.0 | all-reduce | flops 4096 | bytes 32768 | tf_op jit(solution)/shard_map/psum | solution.py:40
  325.0 10.2 %psum.31 = f32[4096]{0:T(1024)S(1)} all-reduce(f32[4096]{0:T(1024)S(1)} %psum.30), channel_id=1, replica_groups=mesh['vocab'=4,'fsdp'=8] {'vocab'}, use_global_device_ids=true, to_apply=%region_11.0 | all-reduce | flops 4096 | bytes 32768 | tf_op jit(solution)/shard_map/psum | solution.py:40
  335.2 0.0 copy-start
  335.2 0.0 copy-start.1
  335.2 33.4 %copy.10 = f32[4096,2048]{1,0:T(8,128)} copy(f32[4096,2048]{0,1:T(8,128)} %get-tuple-element.11) | data formatting | bytes 67108864
  368.6 0.0 copy-done
  368.6 0.0 copy-done.1
  368.6 0.6 fusion.23
  (4 shorter events, 0.0 us)
Async XLA Ops:
  7.2 72.0 %all-gather.7.cloned.1.call-start = ((), (), s32[]{:S(2)}) async-start(), calls=%async_computation | async-start | bytes 3538944 | tf_op jit(solution)/shard_map/all_gather | solution.py:24
  11.7 123.8 %all-gather.9.cloned.1.call-start = ((), (), s32[]{:S(2)}) async-start(), calls=%async_computation.1 | async-start | bytes 3538944 | tf_op jit(solution)/shard_map/all_gather | solution.py:24
  33.4 31.2 %copy-start.3 = (u32[32]{0:T(128)S(1)}, u32[32]{0:T(128)}, u32[]{:S(2)}) copy-start(u32[32]{0:T(128)} %constant.34) | copy-start | bytes 388
  33.4 32.4 %copy-start.2 = (s32[2,48]{1,0:T(2,128)S(1)}, s32[2,48]{1,0:T(2,128)}, u32[]{:S(2)}) copy-start(s32[2,48]{1,0:T(2,128)} %param.8) | copy-start | bytes 1156
  335.2 33.4 %copy-start = (bf16[4096]{0:T(1024)(128)(2,1)S(1)}, bf16[4096]{0:T(1024)(128)(2,1)}, u32[]{:S(2)}) copy-start(bf16[4096]{0:T(1024)(128)(2,1)} %param.7) | copy-start | bytes 24580
  335.2 33.4 %copy-start.1 = (f32[4096]{0:T(1024)S(1)}, f32[4096]{0:T(1024)}, u32[]{:S(2)}) copy-start(f32[4096]{0:T(1024)} %param.11) | copy-start | bytes 49156
Sparse Core Ops, SparseCore 0:
  11.8 62.7 all-gather.6
  76.7 58.7 all-gather.8
